TPU v7x, 32 devices: a whole 2x2x4 slice. The times are simulated.
32 devices in a mesh: mem: 8 (over z, y), band: 4 (over x, core).
Axes of the slice: x: 2, y: 2, z: 4, core: 2. Of those that a mesh axis runs over, the one named last changes fastest.
Arguments:
- ensemble: float32 [256, 256, 256], P('mem', 'band'), may hold values from -8 to 8
- column_operator: float32 [128, 128], replicated, may hold values from -0.5 to 0.5
- patch_order: int32 [4, 64], P('band'), may hold values from 0 to 63, as said below
- obs_index: int32 [4, 64, 512], P('band'), may hold values from 0 to 255
- obs_count: int32 [4, 64], P('band', 'mem'), may hold values from 1 to 512
- obs_values: float32 [4, 64, 512], P('band', 'mem'), may hold values from -8 to 8
- obs_precision: float32 [4, 64, 512], P('band', 'mem'), may hold values from 2 to 50
Outputs:
- analysis: float32 [256, 256, 256], P('mem', 'band')
- transform: float32 [4, 64, 256, 256], P('band', 'mem')
Inputs may be any that keep to these rules, and one draw needn't show every extreme that they name: `patch_order`: each row is a permutation of 0 to 63.
All inputs are finite; a program needn't handle non-finite values.
Results may differ from a plain program's by a relative error of at most 0.0003.
Values sent between devices are 32-bit elements; how exact they have to be, the bound alone decides.
A program may use at most 64 MiB of HBM per device.

v0:
```python
import math
import jax
import jax.numpy as jnp
from jax import lax
from jax.sharding import PartitionSpec as P

ITERS = 12


def batched(left, right):
    return jnp.einsum("pij,pjk->pik", left, right, precision=lax.Precision.HIGHEST)


def map_columns(states, column_operator):
    rows, patches, cells = states.shape
    levels = column_operator.shape[0]
    flat_rows = states.reshape(rows * patches * (cells // levels), levels)
    mapped = jnp.dot(flat_rows, column_operator, precision=lax.Precision.HIGHEST)
    return mapped.reshape(rows, patches, -1)


def select_slots(channel_values, index):
    width = channel_values.shape[2]
    places = jnp.arange(width, dtype=jnp.int32)
    picker = (index[:, None, :] == places[None, :, None]).astype(jnp.float32)
    return jnp.einsum("kpc,pco->kpo", channel_values, picker, precision=lax.Precision.HIGHEST)


def local(ensemble, column_operator, patch_order, obs_index, obs_count, obs_values, obs_precision):
    highest = lax.Precision.HIGHEST
    members_dev, band_patches, cells = ensemble.shape
    slots = obs_index.shape[2]
    n_mem = lax.axis_size("mem")
    worker = lax.axis_index("mem")
    per_worker = band_patches // n_mem
    order = patch_order[0]
    positions = jnp.arange(band_patches, dtype=jnp.int32)
    permuter = (order[None, :] == positions[:, None]).astype(jnp.float32)
    listed = jnp.einsum("kqc,qj->kjc", ensemble, permuter, precision=highest)
    my_index = lax.dynamic_slice_in_dim(obs_index[0], worker * per_worker, per_worker, 0)
    state_in = lax.all_to_all(listed, "mem", split_axis=1, concat_axis=0, tiled=True)
    obs_block = select_slots(map_columns(state_in, column_operator), my_index)
    count = obs_count[0]
    values = obs_values[0]
    precision = obs_precision[0]
    members = obs_block.shape[0]
    live = (jnp.arange(slots, dtype=jnp.int32)[None, :] < count[:, None]).astype(jnp.float32)
    obs_weight = precision * live
    obs_mean = jnp.mean(obs_block, axis=0)
    obs_pert = obs_block - obs_mean
    innov = (values - obs_mean) * obs_weight
    gram = jnp.einsum("kpo,jpo->pkj", obs_pert * obs_weight, obs_pert, precision=highest)
    identity = jnp.eye(members, dtype=jnp.float32)
    system = gram + (members - 1.0) * identity
    trace_value = jnp.trace(system, axis1=1, axis2=2)
    level = system / trace_value[:, None, None]

    def sweep(step, carry):
        ymat, zmat = carry
        turn = 1.5 * identity - 0.5 * batched(zmat, ymat)
        return (batched(ymat, turn), batched(turn, zmat))

    ymat, zmat = lax.fori_loop(0, ITERS, sweep, (level, jnp.broadcast_to(identity, level.shape)))
    root = zmat / jnp.sqrt(trace_value)[:, None, None]
    spread = math.sqrt(members - 1.0) * root
    projected = jnp.einsum("kpo,po->pk", obs_pert, innov, precision=highest)
    inner = jnp.einsum("pij,pj->pi", root, projected, precision=highest)
    mean_weight = jnp.einsum("pij,pj->pi", root, inner, precision=highest)
    coef = spread + mean_weight[:, :, None]
    state_mean = jnp.mean(state_in, axis=0)
    state_pert = state_in - state_mean
    updated = state_mean + jnp.einsum("pjk,jpc->kpc", coef, state_pert, precision=highest)
    returned = lax.all_to_all(updated, "mem", split_axis=0, concat_axis=1, tiled=True)
    restored = jnp.einsum("kjc,qj->kqc", returned, permuter, precision=highest)
    return (restored, spread[None])


def solution(mesh):
    placed = (
        P("mem", "band", None),
        P(),
        P("band", None),
        P("band", None, None),
        P("band", "mem"),
        P("band", "mem", None),
        P("band", "mem", None),
    )
    return jax.shard_map(
        local,
        mesh=mesh,
        in_specs=placed,
        out_specs=(P("mem", "band", None), P("band", "mem", None, None)),
        check_vma=False,
    )
```

profile of v0, /device:TPU:0, one launch (start us, length us, event | category | flops | bytes accessed | tf_op | source)
XLA Modules:
  0.0 328.3 jit_solution(8018955491535311315)
XLA Ops:
  2.2 1.9 convolution_bitcast_fusion
  4.1 2.5 copy.41
  6.7 7.4 %all-to-all-start = ((f32[32,64,256]{2,0,1:T(8,128)}), f32[32,64,256]{2,0,1:T(8,128)}, u32[]{:S(2)}, u32[]{:S(2)}) async-start(f32[32,64,256]{2,0,1:T(8,128)} %copy.41), calls=%async_computation | async-start | bytes 4194304 | tf_op jit(solution)/shard_map/all_to_all | solution.py:41
  15.0 47.5 %all-to-all-done = f32[32,64,256]{2,0,1:T(8,128)} async-done(((f32[32,64,256]{2,0,1:T(8,128)}), f32[32,64,256]{2,0,1:T(8,128)}, u32[]{:S(2)}, u32[]{:S(2)}) %all-to-all-start) | async-done | bytes 2097184 | tf_op jit(solution)/shard_map/all_to_all | solution.py:41
  62.5 4.1 %copy.43 = f32[8,32,8,256]{3,2,1,0:T(8,128)} copy(f32[8,32,8,256]{3,1,2,0:T(8,128)} %bitcast.7) | data formatting | bytes 4194304 | tf_op jit(solution)/shard_map/all_to_all | solution.py:41
  66.6 2.7 bitcast_reduce_fusion.1
  69.2 2.6 reshape.71
  71.9 3.2 bitcast_subtract_fusion.3
  75.1 3.1 fusion.53
  78.2 2.9 reshape.72
  81.1 4.3 %bitcast_reduce_fusion = (f32[8,512]{1,0:T(8,128)S(1)}, f32[8,512,256]{1,2,0:T(8,128)S(1)}) fusion(f32[256,8,256]{2,1,0:T(8,128)} %reshape.72, s32[8,512]{1,0:T(8,128)S(1)} %dynamic-slice_bitcast_fusion), kind=kOutput, calls=%fused_computation.16 | convolution fusion | flops 3223318528 | bytes 6324224 | tf_op jit(solution)/shard_map/kpc,pco->kpo/dot_general | solution.py:26
  85.5 3.7 %fusion.15 = f32[8,1,256]{2,1,0:T(1,128)S(1)} fusion(f32[8,512,256]{1,2,0:T(8,128)S(1)} %get-tuple-element.54, f32[8,512]{1,0:T(8,128)S(1)} %get-tuple-element.52, f32[8,512,1]{1,0,2:T(8,128)S(1)} %get-tuple-element.51), kind=kOutput, calls=%fused_computation.19 | convolution fusion | flops 13631488 | bytes 4235264 | tf_op jit(solution)/shard_map/kpo,po->pk/dot_general | solution.py:66
  89.2 4.7 %select_reduce_fusion = (f32[8]{0:T(128)S(1)}, f32[8,256,256]{2,1,0:T(8,128)S(1)}) fusion(f32[256,256]{1,0:T(8,128)S(1)} %fusion.38, pred[256,256]{1,0:T(8,128)(4,1)S(1)} %iota_compare_fusion.3, f32[8,512,256]{1,2,0:T(8,128)S(1)} %get-tuple-element.54, f32[8,512]{1,0:T(8,128)S(1)} %get-tuple-element.52, f32[8,512]{1,0:T(8,128)S(1)} %select_bitcast_fusion), kind=kOutput, calls=%fused_computation.30 | convolution fusion | flops 3225944064 | bytes 6651936 | tf_op jit(solution)/shard_map/kpo,jpo->pkj/dot_general | solution.py:52
  95.6 2.9 copy.46
  100.0 157.3 %while.13 = (s32[]{:T(128)}, f32[8,256,256]{1,2,0:T(8,128)}, f32[8,256,256]{2,1,0:T(8,128)}, s32[]{:T(128)}) while((s32[]{:T(128)}, f32[8,256,256]{1,2,0:T(8,128)}, f32[8,256,256]{2,1,0:T(8,128)}, s32[]{:T(128)}) %tuple.32), condition=%wide.region_4.5_spmd.clone, body=%wide.region_3.4_spmd.clone.sunk | while | flops 4834066432 | bytes 36438096 | solution.py:63
  100.0 1.7 copy.103
  102.5 2.2 fusion.73
  104.7 4.9 %fusion.75 = f32[8,256,256]{1,2,0:T(8,128)} fusion(f32[8,256,256]{1,2,0:T(8,128)S(1)} %copy.103, f32[8,256,256]{2,1,0:T(8,128)S(1)} %fusion.73, f32[256,256]{1,0:T(8,128)S(1)} %fusion.74), kind=kOutput, calls=%fused_computation.4.clone.1 | convolution fusion | flops 1611661312 | bytes 6553600 | tf_op jit(solution)/shard_map/while/body/eval_jaxpr/pij,pjk->pik/dot_general | solution.py:11
  109.6 3.6 %fusion.76 = f32[8,256,256]{2,1,0:T(8,128)} fusion(f32[8,256,256]{2,1,0:T(8,128)S(1)} %copy.104, f32[8,256,256]{2,1,0:T(8,128)S(1)} %fusion.73, f32[256,256]{1,0:T(8,128)S(1)} %fusion.74), kind=kOutput, calls=%fused_computation.2.clone.1 | convolution fusion | flops 1611661312 | bytes 6553600 | tf_op jit(solution)/shard_map/while/body/eval_jaxpr/pij,pjk->pik/dot_general | solution.py:11
  115.6 2.2 fusion.73
  117.8 4.9 %fusion.75 = f32[8,256,256]{1,2,0:T(8,128)} fusion(f32[8,256,256]{1,2,0:T(8,128)S(1)} %copy.103, f32[8,256,256]{2,1,0:T(8,128)S(1)} %fusion.73, f32[256,256]{1,0:T(8,128)S(1)} %fusion.74), kind=kOutput, calls=%fused_computation.4.clone.1 | convolution fusion | flops 1611661312 | bytes 6553600 | tf_op jit(solution)/shard_map/while/body/eval_jaxpr/pij,pjk->pik/dot_general | solution.py:11
  122.7 3.6 %fusion.76 = f32[8,256,256]{2,1,0:T(8,128)} fusion(f32[8,256,256]{2,1,0:T(8,128)S(1)} %copy.104, f32[8,256,256]{2,1,0:T(8,128)S(1)} %fusion.73, f32[256,256]{1,0:T(8,128)S(1)} %fusion.74), kind=kOutput, calls=%fused_computation.2.clone.1 | convolution fusion | flops 1611661312 | bytes 6553600 | tf_op jit(solution)/shard_map/while/body/eval_jaxpr/pij,pjk->pik/dot_general | solution.py:11
  128.7 2.2 fusion.73
  130.9 4.9 %fusion.75 = f32[8,256,256]{1,2,0:T(8,128)} fusion(f32[8,256,256]{1,2,0:T(8,128)S(1)} %copy.103, f32[8,256,256]{2,1,0:T(8,128)S(1)} %fusion.73, f32[256,256]{1,0:T(8,128)S(1)} %fusion.74), kind=kOutput, calls=%fused_computation.4.clone.1 | convolution fusion | flops 1611661312 | bytes 6553600 | tf_op jit(solution)/shard_map/while/body/eval_jaxpr/pij,pjk->pik/dot_general | solution.py:11
  135.8 3.6 %fusion.76 = f32[8,256,256]{2,1,0:T(8,128)} fusion(f32[8,256,256]{2,1,0:T(8,128)S(1)} %copy.104, f32[8,256,256]{2,1,0:T(8,128)S(1)} %fusion.73, f32[256,256]{1,0:T(8,128)S(1)} %fusion.74), kind=kOutput, calls=%fused_computation.2.clone.1 | convolution fusion | flops 1611661312 | bytes 6553600 | tf_op jit(solution)/shard_map/while/body/eval_jaxpr/pij,pjk->pik/dot_general | solution.py:11
  139.3 1.7 copy.103
  141.8 2.2 fusion.73
  144.0 4.9 %fusion.75 = f32[8,256,256]{1,2,0:T(8,128)} fusion(f32[8,256,256]{1,2,0:T(8,128)S(1)} %copy.103, f32[8,256,256]{2,1,0:T(8,128)S(1)} %fusion.73, f32[256,256]{1,0:T(8,128)S(1)} %fusion.74), kind=kOutput, calls=%fused_computation.4.clone.1 | convolution fusion | flops 1611661312 | bytes 6553600 | tf_op jit(solution)/shard_map/while/body/eval_jaxpr/pij,pjk->pik/dot_general | solution.py:11
  148.9 3.6 %fusion.76 = f32[8,256,256]{2,1,0:T(8,128)} fusion(f32[8,256,256]{2,1,0:T(8,128)S(1)} %copy.104, f32[8,256,256]{2,1,0:T(8,128)S(1)} %fusion.73, f32[256,256]{1,0:T(8,128)S(1)} %fusion.74), kind=kOutput, calls=%fused_computation.2.clone.1 | convolution fusion | flops 1611661312 | bytes 6553600 | tf_op jit(solution)/shard_map/while/body/eval_jaxpr/pij,pjk->pik/dot_general | solution.py:11
  152.5 1.7 copy.103
  154.9 2.2 fusion.73
  157.1 4.9 %fusion.75 = f32[8,256,256]{1,2,0:T(8,128)} fusion(f32[8,256,256]{1,2,0:T(8,128)S(1)} %copy.103, f32[8,256,256]{2,1,0:T(8,128)S(1)} %fusion.73, f32[256,256]{1,0:T(8,128)S(1)} %fusion.74), kind=kOutput, calls=%fused_computation.4.clone.1 | convolution fusion | flops 1611661312 | bytes 6553600 | tf_op jit(solution)/shard_map/while/body/eval_jaxpr/pij,pjk->pik/dot_general | solution.py:11
  162.0 3.6 %fusion.76 = f32[8,256,256]{2,1,0:T(8,128)} fusion(f32[8,256,256]{2,1,0:T(8,128)S(1)} %copy.104, f32[8,256,256]{2,1,0:T(8,128)S(1)} %fusion.73, f32[256,256]{1,0:T(8,128)S(1)} %fusion.74), kind=kOutput, calls=%fused_computation.2.clone.1 | convolution fusion | flops 1611661312 | bytes 6553600 | tf_op jit(solution)/shard_map/while/body/eval_jaxpr/pij,pjk->pik/dot_general | solution.py:11
  168.0 2.2 fusion.73
  170.2 4.9 %fusion.75 = f32[8,256,256]{1,2,0:T(8,128)} fusion(f32[8,256,256]{1,2,0:T(8,128)S(1)} %copy.103, f32[8,256,256]{2,1,0:T(8,128)S(1)} %fusion.73, f32[256,256]{1,0:T(8,128)S(1)} %fusion.74), kind=kOutput, calls=%fused_computation.4.clone.1 | convolution fusion | flops 1611661312 | bytes 6553600 | tf_op jit(solution)/shard_map/while/body/eval_jaxpr/pij,pjk->pik/dot_general | solution.py:11
  175.1 3.6 %fusion.76 = f32[8,256,256]{2,1,0:T(8,128)} fusion(f32[8,256,256]{2,1,0:T(8,128)S(1)} %copy.104, f32[8,256,256]{2,1,0:T(8,128)S(1)} %fusion.73, f32[256,256]{1,0:T(8,128)S(1)} %fusion.74), kind=kOutput, calls=%fused_computation.2.clone.1 | convolution fusion | flops 1611661312 | bytes 6553600 | tf_op jit(solution)/shard_map/while/body/eval_jaxpr/pij,pjk->pik/dot_general | solution.py:11
  178.7 1.7 copy.103
  181.1 2.2 fusion.73
  183.3 4.9 %fusion.75 = f32[8,256,256]{1,2,0:T(8,128)} fusion(f32[8,256,256]{1,2,0:T(8,128)S(1)} %copy.103, f32[8,256,256]{2,1,0:T(8,128)S(1)} %fusion.73, f32[256,256]{1,0:T(8,128)S(1)} %fusion.74), kind=kOutput, calls=%fused_computation.4.clone.1 | convolution fusion | flops 1611661312 | bytes 6553600 | tf_op jit(solution)/shard_map/while/body/eval_jaxpr/pij,pjk->pik/dot_general | solution.py:11
  188.2 3.6 %fusion.76 = f32[8,256,256]{2,1,0:T(8,128)} fusion(f32[8,256,256]{2,1,0:T(8,128)S(1)} %copy.104, f32[8,256,256]{2,1,0:T(8,128)S(1)} %fusion.73, f32[256,256]{1,0:T(8,128)S(1)} %fusion.74), kind=kOutput, calls=%fused_computation.2.clone.1 | convolution fusion | flops 1611661312 | bytes 6553600 | tf_op jit(solution)/shard_map/while/body/eval_jaxpr/pij,pjk->pik/dot_general | solution.py:11
  194.2 2.2 fusion.73
  196.4 4.9 %fusion.75 = f32[8,256,256]{1,2,0:T(8,128)} fusion(f32[8,256,256]{1,2,0:T(8,128)S(1)} %copy.103, f32[8,256,256]{2,1,0:T(8,128)S(1)} %fusion.73, f32[256,256]{1,0:T(8,128)S(1)} %fusion.74), kind=kOutput, calls=%fused_computation.4.clone.1 | convolution fusion | flops 1611661312 | bytes 6553600 | tf_op jit(solution)/shard_map/while/body/eval_jaxpr/pij,pjk->pik/dot_general | solution.py:11
  201.3 3.6 %fusion.76 = f32[8,256,256]{2,1,0:T(8,128)} fusion(f32[8,256,256]{2,1,0:T(8,128)S(1)} %copy.104, f32[8,256,256]{2,1,0:T(8,128)S(1)} %fusion.73, f32[256,256]{1,0:T(8,128)S(1)} %fusion.74), kind=kOutput, calls=%fused_computation.2.clone.1 | convolution fusion | flops 1611661312 | bytes 6553600 | tf_op jit(solution)/shard_map/while/body/eval_jaxpr/pij,pjk->pik/dot_general | solution.py:11
  204.9 1.7 copy.103
  207.4 2.2 fusion.73
  209.5 4.9 %fusion.75 = f32[8,256,256]{1,2,0:T(8,128)} fusion(f32[8,256,256]{1,2,0:T(8,128)S(1)} %copy.103, f32[8,256,256]{2,1,0:T(8,128)S(1)} %fusion.73, f32[256,256]{1,0:T(8,128)S(1)} %fusion.74), kind=kOutput, calls=%fused_computation.4.clone.1 | convolution fusion | flops 1611661312 | bytes 6553600 | tf_op jit(solution)/shard_map/while/body/eval_jaxpr/pij,pjk->pik/dot_general | solution.py:11
  214.5 3.6 %fusion.76 = f32[8,256,256]{2,1,0:T(8,128)} fusion(f32[8,256,256]{2,1,0:T(8,128)S(1)} %copy.104, f32[8,256,256]{2,1,0:T(8,128)S(1)} %fusion.73, f32[256,256]{1,0:T(8,128)S(1)} %fusion.74), kind=kOutput, calls=%fused_computation.2.clone.1 | convolution fusion | flops 1611661312 | bytes 6553600 | tf_op jit(solution)/shard_map/while/body/eval_jaxpr/pij,pjk->pik/dot_general | solution.py:11
  220.5 2.2 fusion.73
  222.7 4.9 %fusion.75 = f32[8,256,256]{1,2,0:T(8,128)} fusion(f32[8,256,256]{1,2,0:T(8,128)S(1)} %copy.103, f32[8,256,256]{2,1,0:T(8,128)S(1)} %fusion.73, f32[256,256]{1,0:T(8,128)S(1)} %fusion.74), kind=kOutput, calls=%fused_computation.4.clone.1 | convolution fusion | flops 1611661312 | bytes 6553600 | tf_op jit(solution)/shard_map/while/body/eval_jaxpr/pij,pjk->pik/dot_general | solution.py:11
  227.6 3.6 %fusion.76 = f32[8,256,256]{2,1,0:T(8,128)} fusion(f32[8,256,256]{2,1,0:T(8,128)S(1)} %copy.104, f32[8,256,256]{2,1,0:T(8,128)S(1)} %fusion.73, f32[256,256]{1,0:T(8,128)S(1)} %fusion.74), kind=kOutput, calls=%fused_computation.2.clone.1 | convolution fusion | flops 1611661312 | bytes 6553600 | tf_op jit(solution)/shard_map/while/body/eval_jaxpr/pij,pjk->pik/dot_general | solution.py:11
  233.6 2.2 fusion.73
  235.8 4.9 %fusion.75 = f32[8,256,256]{1,2,0:T(8,128)} fusion(f32[8,256,256]{1,2,0:T(8,128)S(1)} %copy.103, f32[8,256,256]{2,1,0:T(8,128)S(1)} %fusion.73, f32[256,256]{1,0:T(8,128)S(1)} %fusion.74), kind=kOutput, calls=%fused_computation.4.clone.1 | convolution fusion | flops 1611661312 | bytes 6553600 | tf_op jit(solution)/shard_map/while/body/eval_jaxpr/pij,pjk->pik/dot_general | solution.py:11
  240.7 3.6 %fusion.76 = f32[8,256,256]{2,1,0:T(8,128)} fusion(f32[8,256,256]{2,1,0:T(8,128)S(1)} %copy.104, f32[8,256,256]{2,1,0:T(8,128)S(1)} %fusion.73, f32[256,256]{1,0:T(8,128)S(1)} %fusion.74), kind=kOutput, calls=%fused_computation.2.clone.1 | convolution fusion | flops 1611661312 | bytes 6553600 | tf_op jit(solution)/shard_map/while/body/eval_jaxpr/pij,pjk->pik/dot_general | solution.py:11
  246.7 2.2 fusion.73
  248.9 4.9 %fusion.75 = f32[8,256,256]{1,2,0:T(8,128)} fusion(f32[8,256,256]{1,2,0:T(8,128)S(1)} %copy.103, f32[8,256,256]{2,1,0:T(8,128)S(1)} %fusion.73, f32[256,256]{1,0:T(8,128)S(1)} %fusion.74), kind=kOutput, calls=%fused_computation.4.clone.1 | convolution fusion | flops 1611661312 | bytes 6553600 | tf_op jit(solution)/shard_map/while/body/eval_jaxpr/pij,pjk->pik/dot_general | solution.py:11
  253.8 3.6 %fusion.76 = f32[8,256,256]{2,1,0:T(8,128)} fusion(f32[8,256,256]{2,1,0:T(8,128)S(1)} %copy.104, f32[8,256,256]{2,1,0:T(8,128)S(1)} %fusion.73, f32[256,256]{1,0:T(8,128)S(1)} %fusion.74), kind=kOutput, calls=%fused_computation.2.clone.1 | convolution fusion | flops 1611661312 | bytes 6553600 | tf_op jit(solution)/shard_map/while/body/eval_jaxpr/pij,pjk->pik/dot_general | solution.py:11
  257.4 3.7 %fusion.49 = f32[8,1,256]{2,1,0:T(1,128)S(1)} fusion(f32[8,256,1]{1,0,2:T(8,128)S(1)} %bitcast.90, f32[8,256,256]{2,1,0:T(8,128)} %get-tuple-element.24, f32[8]{0:T(128)S(1)} %sqrt.7), kind=kOutput, calls=%fused_computation.63 | convolution fusion | flops 6815744 | bytes 2113568 | tf_op jit(solution)/shard_map/pij,pj->pi/dot_general | solution.py:67
  261.1 2.0 fusion.47
  263.1 5.9 %add_bitcast_fusion = f32[256,8,256]{0,2,1:T(8,128)} fusion(f32[256,8,256]{2,1,0:T(8,128)S(1)} %copy-done.4, f32[8,256]{1,0:T(8,128)S(1)} %bitcast.91, f32[8,256]{1,0:T(8,128)S(1)} %broadcast_multiply_fusion.1, f32[8,256,256]{2,1,0:T(8,128)S(1)} %copy-done.2, f32[8]{0:T(128)S(1)} %sqrt.7), kind=kOutput, calls=%fused_computation.28 | convolution fusion | flops 1612709888 | bytes 6307872 | tf_op jit(solution)/shard_map/pjk,jpc->kpc/dot_general | solution.py:72
  269.0 3.1 copy.48
  272.0 4.3 %all-to-all-start.1 = ((f32[256,8,256]{2,1,0:T(8,128)}), f32[256,8,256]{2,1,0:T(8,128)}, u32[]{:S(2)}, u32[]{:S(2)}) async-start(f32[256,8,256]{2,1,0:T(8,128)} %copy.48), calls=%async_computation.1 | async-start | bytes 4194304 | tf_op jit(solution)/shard_map/all_to_all | solution.py:73
  276.4 3.2 multiply_bitcast_fusion
  279.6 44.6 %all-to-all-done.1 = f32[256,8,256]{2,1,0:T(8,128)} async-done(((f32[256,8,256]{2,1,0:T(8,128)}), f32[256,8,256]{2,1,0:T(8,128)}, u32[]{:S(2)}, u32[]{:S(2)}) %all-to-all-start.1) | async-done | bytes 2097184 | tf_op jit(solution)/shard_map/all_to_all | solution.py:73
  324.2 4.1 %fusion.32 = f32[32,64,256]{2,1,0:T(8,128)} fusion(f32[32,8,8,256]{3,2,0,1:T(8,128)} %bitcast.24, s32[64]{0:T(128)S(1)} %bitcast.96), kind=kOutput, calls=%fused_computation.38 | convolution fusion | flops 402657280 | bytes 4194560 | tf_op jit(solution)/shard_map/kjc,qj->kqc/dot_general | solution.py:74
  (86 shorter events, 26.5 us)
Async XLA Ops:
  0.6 1.6 copy-start
  6.7 8.2 %copy-start.6 = (f32[1,8,512]{2,1,0:T(8,128)S(1)}, f32[1,8,512]{2,1,0:T(8,128)}, u32[]{:S(2)}) copy-start(f32[1,8,512]{2,1,0:T(8,128)} %param.15) | copy-start | bytes 49156
  6.7 8.3 %copy-start.8 = (s32[1,8]{1,0:T(1,128)S(1)}, s32[1,8]{1,0:T(1,128)}, u32[]{:S(2)}) copy-start(s32[1,8]{1,0:T(1,128)} %param.13) | copy-start | bytes 100
  6.7 55.8 %all-to-all-start = ((f32[32,64,256]{2,0,1:T(8,128)}), f32[32,64,256]{2,0,1:T(8,128)}, u32[]{:S(2)}, u32[]{:S(2)}) async-start(f32[32,64,256]{2,0,1:T(8,128)} %copy.41), calls=%async_computation | async-start | bytes 4194304 | tf_op jit(solution)/shard_map/all_to_all | solution.py:41
  71.9 3.2 copy-start.3
  71.9 3.2 copy-start.5
  81.1 4.3 %copy-start.7 = (f32[1,8,512]{2,1,0:T(8,128)S(1)}, f32[1,8,512]{2,1,0:T(8,128)}, u32[]{:S(2)}) copy-start(f32[1,8,512]{2,1,0:T(8,128)} %param.14) | copy-start | bytes 49156
  100.0 2.2 copy-start.1
  113.1 2.2 copy-start.1
  126.2 2.2 copy-start.1
  139.3 2.2 copy-start.1
  152.5 2.2 copy-start.1
  165.6 2.2 copy-start.1
  178.7 2.2 copy-start.1
  191.8 2.2 copy-start.1
  204.9 2.2 copy-start.1
  218.0 2.2 copy-start.1
  231.1 2.2 copy-start.1
  244.2 2.2 copy-start.1
  257.3 3.7 %copy-start.2 = (f32[8,256,256]{2,1,0:T(8,128)S(1)}, f32[8,256,256]{2,1,0:T(8,128)}, u32[]{:S(2)}) copy-start(f32[8,256,256]{2,1,0:T(8,128)} %get-tuple-element.24) | copy-start | bytes 6291460
  261.1 2.0 copy-start.4
  272.0 52.2 %all-to-all-start.1 = ((f32[256,8,256]{2,1,0:T(8,128)}), f32[256,8,256]{2,1,0:T(8,128)}, u32[]{:S(2)}, u32[]{:S(2)}) async-start(f32[256,8,256]{2,1,0:T(8,128)} %copy.48), calls=%async_computation.1 | async-start | bytes 4194304 | tf_op jit(solution)/shard_map/all_to_all | solution.py:73
  276.4 47.8 %copy-start.9 = (s32[1,64]{1,0:T(1,128)S(1)}, s32[1,64]{1,0:T(1,128)}, u32[]{:S(2)}) copy-start(s32[1,64]{1,0:T(1,128)} %param.11) | copy-start | bytes 772
where the time goes:
time: 329 us; the launch traced here: 328 us
  matrix products  161 us (49%)
  waiting for transfers between devices  92 us (28%)
  local copies, waits for them, and re-layouts  51.3 us (16%)
  starting transfers between devices  11.8 us (4%)
  other arithmetic  11.2 us (3%)
    dot_general x36, matrix products, batched(): jnp.einsum('pij,pjk->pik', left, right, precision=lax.Precision.HIGHEST)  128 us
    all_to_all x1, waiting for transfers between devices, local(): lax.all_to_all(listed, 'mem', split_axis=1, concat_axis=0, tiled=True)  47.5 us
    all_to_all x1, waiting for transfers between devices, local(): lax.all_to_all(updated, 'mem', split_axis=0, concat_axis=1, tiled=True)  44.6 us
    while x48, local copies, waits for them, and re-layouts  29.3 us
    all_to_all x1, starting transfers between devices, local(): lax.all_to_all(listed, 'mem', split_axis=1, concat_axis=0, tiled=True)  7.44 us
  transfers between devices with their start and end apart: 2, of which 2 were waited for; matrix products, arithmetic and copies ran while one was open for 1% of the time, Pallas kernels for 0%

commit v1 on v0

--- a/solution.py
+++ b/solution.py
@@ -38,7 +38,10 @@
     permuter = (order[None, :] == positions[:, None]).astype(jnp.float32)
     listed = jnp.einsum("kqc,qj->kjc", ensemble, permuter, precision=highest)
     my_index = lax.dynamic_slice_in_dim(obs_index[0], worker * per_worker, per_worker, 0)
-    state_in = lax.all_to_all(listed, "mem", split_axis=1, concat_axis=0, tiled=True)
+    state_in = jnp.concatenate(
+        lax.all_to_all(jnp.stack(jnp.split(listed, lax.axis_size("mem"), axis=1)), "mem", 0, 0),
+        axis=0,
+    )
     obs_block = select_slots(map_columns(state_in, column_operator), my_index)
     count = obs_count[0]
     values = obs_values[0]

time: 329 us -> 327 us (level)
  other arithmetic: 11.2 us -> 7.19 us
    unnamed x19 -> x24, local copies, waits for them, and re-layouts: 4.56 us -> 9.61 us
    all_to_all x1 -> x0, local copies, waits for them, and re-layouts: 4.1 us -> none  [local(): lax.all_to_all(listed, 'mem', split_axis=1, concat_axis=0, tiled=True)]
    another operation x0 -> x2, local copies, waits for them, and re-layouts: none -> 3.36 us  [the longest x1 2.64 us: map_columns(): flat_rows = states.reshape(rows * patches * (cells // levels), levels)]
where the time goes in v1:
time: 327 us; the launch traced here: 326 us
  matrix products  161 us (49%)
  waiting for transfers between devices  92 us (28%)
  local copies, waits for them, and re-layouts  53.3 us (16%)
  starting transfers between devices  11.8 us (4%)
  other arithmetic  7.19 us (2%)
    dot_general x36, matrix products, batched(): jnp.einsum('pij,pjk->pik', left, right, precision=lax.Precision.HIGHEST)  128 us
    all_to_all x1, waiting for transfers between devices, local(): lax.all_to_all(jnp.stack(jnp.split(listed, lax.axis_size('mem'), axis=1))...  47.5 us
    all_to_all x1, waiting for transfers between devices, local(): lax.all_to_all(updated, 'mem', split_axis=0, concat_axis=1, tiled=True)  44.6 us
    while x48, local copies, waits for them, and re-layouts  29.3 us
    unnamed x24, local copies, waits for them, and re-layouts  9.61 us
    all_to_all x1, starting transfers between devices, local(): lax.all_to_all(jnp.stack(jnp.split(listed, lax.axis_size('mem'), axis=1))...  7.44 us
  transfers between devices with their start and end apart: 2, of which 2 were waited for; matrix products, arithmetic and copies ran while one was open for 1% of the time, Pallas kernels for 0%

profile of v1, /device:TPU:0, one launch (start us, length us, event | category | flops | bytes accessed | tf_op | source)
XLA Modules:
  0.0 326.1 jit_solution(5703119997916158694)
XLA Ops:
  2.2 1.9 convolution_bitcast_fusion
  9.9 7.4 %all-to-all-start = ((f32[8,32,8,256]{3,2,1,0:T(8,128)}), f32[8,32,8,256]{3,2,1,0:T(8,128)}, u32[]{:S(2)}, u32[]{:S(2)}) async-start(f32[8,32,8,256]{3,2,1,0:T(8,128)} %fusion.38), calls=%async_computation | async-start | bytes 4194304 | tf_op jit(solution)/shard_map/all_to_all | solution.py:42
  18.2 47.5 %all-to-all-done = f32[8,32,8,256]{3,2,1,0:T(8,128)} async-done(((f32[8,32,8,256]{3,2,1,0:T(8,128)}), f32[8,32,8,256]{3,2,1,0:T(8,128)}, u32[]{:S(2)}, u32[]{:S(2)}) %all-to-all-start) | async-done | bytes 2097184 | tf_op jit(solution)/shard_map/all_to_all | solution.py:42
  65.7 1.9 reduce_sum.28
  67.6 2.9 copy.30
  70.4 2.6 reshape_reshape.3
  73.1 4.7 %fusion.62 = f32[4096,128]{1,0:T(8,128)} fusion(f32[4096,128]{1,0:T(8,128)} %reshape_reshape.3, f32[128,128]{1,0:T(8,128)S(1)} %copy-done.4), kind=kOutput, calls=%fused_computation.85 | convolution fusion | flops 805306368 | bytes 4259840 | tf_op jit(solution)/shard_map/dot_general | solution.py:18
  77.8 2.9 reshape.71
  80.7 4.3 %bitcast_reduce_fusion = (f32[8,512]{1,0:T(8,128)S(1)}, f32[8,512,256]{1,2,0:T(8,128)S(1)}) fusion(f32[256,8,256]{2,1,0:T(8,128)} %reshape.71, s32[8,512]{1,0:T(8,128)S(1)} %dynamic-slice_bitcast_fusion), kind=kOutput, calls=%fused_computation.16 | convolution fusion | flops 3223318528 | bytes 6324224 | tf_op jit(solution)/shard_map/kpc,pco->kpo/dot_general | solution.py:26
  85.1 3.7 %fusion.15 = f32[8,1,256]{2,1,0:T(1,128)S(1)} fusion(f32[8,512,256]{1,2,0:T(8,128)S(1)} %get-tuple-element.51, f32[8,512]{1,0:T(8,128)S(1)} %get-tuple-element.49, f32[8,512,1]{1,0,2:T(8,128)S(1)} %get-tuple-element.48), kind=kOutput, calls=%fused_computation.19 | convolution fusion | flops 13631488 | bytes 4235264 | tf_op jit(solution)/shard_map/kpo,po->pk/dot_general | solution.py:69
  88.8 4.7 %select_reduce_fusion = (f32[8]{0:T(128)S(1)}, f32[8,256,256]{2,1,0:T(8,128)S(1)}) fusion(f32[256,256]{1,0:T(8,128)S(1)} %fusion.47, pred[256,256]{1,0:T(8,128)(4,1)S(1)} %iota_compare_fusion.3, f32[8,512,256]{1,2,0:T(8,128)S(1)} %get-tuple-element.51, f32[8,512]{1,0:T(8,128)S(1)} %get-tuple-element.49, f32[8,512]{1,0:T(8,128)S(1)} %select_bitcast_fusion), kind=kOutput, calls=%fused_computation.27 | convolution fusion | flops 3225944064 | bytes 6651936 | tf_op jit(solution)/shard_map/kpo,jpo->pkj/dot_general | solution.py:55
  95.2 2.9 copy.32
  99.6 157.3 %while.13 = (s32[]{:T(128)}, f32[8,256,256]{1,2,0:T(8,128)}, f32[8,256,256]{2,1,0:T(8,128)}, s32[]{:T(128)}) while((s32[]{:T(128)}, f32[8,256,256]{1,2,0:T(8,128)}, f32[8,256,256]{2,1,0:T(8,128)}, s32[]{:T(128)}) %tuple.31), condition=%wide.region_4.5_spmd.clone, body=%wide.region_3.4_spmd.clone.sunk | while | flops 4834066432 | bytes 36438096 | solution.py:66
  99.6 1.7 copy.88
  102.1 2.2 fusion.82
  104.2 3.6 %fusion.85 = f32[8,256,256]{2,1,0:T(8,128)} fusion(f32[8,256,256]{2,1,0:T(8,128)S(1)} %copy.89, f32[8,256,256]{2,1,0:T(8,128)S(1)} %fusion.82, f32[256,256]{1,0:T(8,128)S(1)} %fusion.83), kind=kOutput, calls=%fused_computation.2.clone.1 | convolution fusion | flops 1611661312 | bytes 6553600 | tf_op jit(solution)/shard_map/while/body/eval_jaxpr/pij,pjk->pik/dot_general | solution.py:11
  107.8 4.9 %fusion.84 = f32[8,256,256]{1,2,0:T(8,128)} fusion(f32[8,256,256]{1,2,0:T(8,128)S(1)} %copy.88, f32[8,256,256]{2,1,0:T(8,128)S(1)} %fusion.82, f32[256,256]{1,0:T(8,128)S(1)} %fusion.83), kind=kOutput, calls=%fused_computation.4.clone.1 | convolution fusion | flops 1611661312 | bytes 6553600 | tf_op jit(solution)/shard_map/while/body/eval_jaxpr/pij,pjk->pik/dot_general | solution.py:11
  112.7 1.7 copy.88
  115.2 2.2 fusion.82
  117.3 3.6 %fusion.85 = f32[8,256,256]{2,1,0:T(8,128)} fusion(f32[8,256,256]{2,1,0:T(8,128)S(1)} %copy.89, f32[8,256,256]{2,1,0:T(8,128)S(1)} %fusion.82, f32[256,256]{1,0:T(8,128)S(1)} %fusion.83), kind=kOutput, calls=%fused_computation.2.clone.1 | convolution fusion | flops 1611661312 | bytes 6553600 | tf_op jit(solution)/shard_map/while/body/eval_jaxpr/pij,pjk->pik/dot_general | solution.py:11
  120.9 4.9 %fusion.84 = f32[8,256,256]{1,2,0:T(8,128)} fusion(f32[8,256,256]{1,2,0:T(8,128)S(1)} %copy.88, f32[8,256,256]{2,1,0:T(8,128)S(1)} %fusion.82, f32[256,256]{1,0:T(8,128)S(1)} %fusion.83), kind=kOutput, calls=%fused_computation.4.clone.1 | convolution fusion | flops 1611661312 | bytes 6553600 | tf_op jit(solution)/shard_map/while/body/eval_jaxpr/pij,pjk->pik/dot_general | solution.py:11
  125.8 1.7 copy.88
  128.3 2.2 fusion.82
  130.5 3.6 %fusion.85 = f32[8,256,256]{2,1,0:T(8,128)} fusion(f32[8,256,256]{2,1,0:T(8,128)S(1)} %copy.89, f32[8,256,256]{2,1,0:T(8,128)S(1)} %fusion.82, f32[256,256]{1,0:T(8,128)S(1)} %fusion.83), kind=kOutput, calls=%fused_computation.2.clone.1 | convolution fusion | flops 1611661312 | bytes 6553600 | tf_op jit(solution)/shard_map/while/body/eval_jaxpr/pij,pjk->pik/dot_general | solution.py:11
  134.0 4.9 %fusion.84 = f32[8,256,256]{1,2,0:T(8,128)} fusion(f32[8,256,256]{1,2,0:T(8,128)S(1)} %copy.88, f32[8,256,256]{2,1,0:T(8,128)S(1)} %fusion.82, f32[256,256]{1,0:T(8,128)S(1)} %fusion.83), kind=kOutput, calls=%fused_computation.4.clone.1 | convolution fusion | flops 1611661312 | bytes 6553600 | tf_op jit(solution)/shard_map/while/body/eval_jaxpr/pij,pjk->pik/dot_general | solution.py:11
  138.9 1.7 copy.88
  141.4 2.2 fusion.82
  143.6 3.6 %fusion.85 = f32[8,256,256]{2,1,0:T(8,128)} fusion(f32[8,256,256]{2,1,0:T(8,128)S(1)} %copy.89, f32[8,256,256]{2,1,0:T(8,128)S(1)} %fusion.82, f32[256,256]{1,0:T(8,128)S(1)} %fusion.83), kind=kOutput, calls=%fused_computation.2.clone.1 | convolution fusion | flops 1611661312 | bytes 6553600 | tf_op jit(solution)/shard_map/while/body/eval_jaxpr/pij,pjk->pik/dot_general | solution.py:11
  147.1 4.9 %fusion.84 = f32[8,256,256]{1,2,0:T(8,128)} fusion(f32[8,256,256]{1,2,0:T(8,128)S(1)} %copy.88, f32[8,256,256]{2,1,0:T(8,128)S(1)} %fusion.82, f32[256,256]{1,0:T(8,128)S(1)} %fusion.83), kind=kOutput, calls=%fused_computation.4.clone.1 | convolution fusion | flops 1611661312 | bytes 6553600 | tf_op jit(solution)/shard_map/while/body/eval_jaxpr/pij,pjk->pik/dot_general | solution.py:11
  152.0 1.7 copy.88
  154.5 2.2 fusion.82
  156.7 3.6 %fusion.85 = f32[8,256,256]{2,1,0:T(8,128)} fusion(f32[8,256,256]{2,1,0:T(8,128)S(1)} %copy.89, f32[8,256,256]{2,1,0:T(8,128)S(1)} %fusion.82, f32[256,256]{1,0:T(8,128)S(1)} %fusion.83), kind=kOutput, calls=%fused_computation.2.clone.1 | convolution fusion | flops 1611661312 | bytes 6553600 | tf_op jit(solution)/shard_map/while/body/eval_jaxpr/pij,pjk->pik/dot_general | solution.py:11
  160.2 4.9 %fusion.84 = f32[8,256,256]{1,2,0:T(8,128)} fusion(f32[8,256,256]{1,2,0:T(8,128)S(1)} %copy.88, f32[8,256,256]{2,1,0:T(8,128)S(1)} %fusion.82, f32[256,256]{1,0:T(8,128)S(1)} %fusion.83), kind=kOutput, calls=%fused_computation.4.clone.1 | convolution fusion | flops 1611661312 | bytes 6553600 | tf_op jit(solution)/shard_map/while/body/eval_jaxpr/pij,pjk->pik/dot_general | solution.py:11
  165.2 1.7 copy.88
  167.6 2.2 fusion.82
  169.8 3.6 %fusion.85 = f32[8,256,256]{2,1,0:T(8,128)} fusion(f32[8,256,256]{2,1,0:T(8,128)S(1)} %copy.89, f32[8,256,256]{2,1,0:T(8,128)S(1)} %fusion.82, f32[256,256]{1,0:T(8,128)S(1)} %fusion.83), kind=kOutput, calls=%fused_computation.2.clone.1 | convolution fusion | flops 1611661312 | bytes 6553600 | tf_op jit(solution)/shard_map/while/body/eval_jaxpr/pij,pjk->pik/dot_general | solution.py:11
  173.4 4.9 %fusion.84 = f32[8,256,256]{1,2,0:T(8,128)} fusion(f32[8,256,256]{1,2,0:T(8,128)S(1)} %copy.88, f32[8,256,256]{2,1,0:T(8,128)S(1)} %fusion.82, f32[256,256]{1,0:T(8,128)S(1)} %fusion.83), kind=kOutput, calls=%fused_computation.4.clone.1 | convolution fusion | flops 1611661312 | bytes 6553600 | tf_op jit(solution)/shard_map/while/body/eval_jaxpr/pij,pjk->pik/dot_general | solution.py:11
  178.3 1.7 copy.88
  180.7 2.2 fusion.82
  182.9 3.6 %fusion.85 = f32[8,256,256]{2,1,0:T(8,128)} fusion(f32[8,256,256]{2,1,0:T(8,128)S(1)} %copy.89, f32[8,256,256]{2,1,0:T(8,128)S(1)} %fusion.82, f32[256,256]{1,0:T(8,128)S(1)} %fusion.83), kind=kOutput, calls=%fused_computation.2.clone.1 | convolution fusion | flops 1611661312 | bytes 6553600 | tf_op jit(solution)/shard_map/while/body/eval_jaxpr/pij,pjk->pik/dot_general | solution.py:11
  186.5 4.9 %fusion.84 = f32[8,256,256]{1,2,0:T(8,128)} fusion(f32[8,256,256]{1,2,0:T(8,128)S(1)} %copy.88, f32[8,256,256]{2,1,0:T(8,128)S(1)} %fusion.82, f32[256,256]{1,0:T(8,128)S(1)} %fusion.83), kind=kOutput, calls=%fused_computation.4.clone.1 | convolution fusion | flops 1611661312 | bytes 6553600 | tf_op jit(solution)/shard_map/while/body/eval_jaxpr/pij,pjk->pik/dot_general | solution.py:11
  193.9 2.2 fusion.82
  196.0 3.6 %fusion.85 = f32[8,256,256]{2,1,0:T(8,128)} fusion(f32[8,256,256]{2,1,0:T(8,128)S(1)} %copy.89, f32[8,256,256]{2,1,0:T(8,128)S(1)} %fusion.82, f32[256,256]{1,0:T(8,128)S(1)} %fusion.83), kind=kOutput, calls=%fused_computation.2.clone.1 | convolution fusion | flops 1611661312 | bytes 6553600 | tf_op jit(solution)/shard_map/while/body/eval_jaxpr/pij,pjk->pik/dot_general | solution.py:11
  199.6 4.9 %fusion.84 = f32[8,256,256]{1,2,0:T(8,128)} fusion(f32[8,256,256]{1,2,0:T(8,128)S(1)} %copy.88, f32[8,256,256]{2,1,0:T(8,128)S(1)} %fusion.82, f32[256,256]{1,0:T(8,128)S(1)} %fusion.83), kind=kOutput, calls=%fused_computation.4.clone.1 | convolution fusion | flops 1611661312 | bytes 6553600 | tf_op jit(solution)/shard_map/while/body/eval_jaxpr/pij,pjk->pik/dot_general | solution.py:11
  207.0 2.2 fusion.82
  209.1 3.6 %fusion.85 = f32[8,256,256]{2,1,0:T(8,128)} fusion(f32[8,256,256]{2,1,0:T(8,128)S(1)} %copy.89, f32[8,256,256]{2,1,0:T(8,128)S(1)} %fusion.82, f32[256,256]{1,0:T(8,128)S(1)} %fusion.83), kind=kOutput, calls=%fused_computation.2.clone.1 | convolution fusion | flops 1611661312 | bytes 6553600 | tf_op jit(solution)/shard_map/while/body/eval_jaxpr/pij,pjk->pik/dot_general | solution.py:11
  212.7 4.9 %fusion.84 = f32[8,256,256]{1,2,0:T(8,128)} fusion(f32[8,256,256]{1,2,0:T(8,128)S(1)} %copy.88, f32[8,256,256]{2,1,0:T(8,128)S(1)} %fusion.82, f32[256,256]{1,0:T(8,128)S(1)} %fusion.83), kind=kOutput, calls=%fused_computation.4.clone.1 | convolution fusion | flops 1611661312 | bytes 6553600 | tf_op jit(solution)/shard_map/while/body/eval_jaxpr/pij,pjk->pik/dot_general | solution.py:11
  220.1 2.2 fusion.82
  222.2 3.6 %fusion.85 = f32[8,256,256]{2,1,0:T(8,128)} fusion(f32[8,256,256]{2,1,0:T(8,128)S(1)} %copy.89, f32[8,256,256]{2,1,0:T(8,128)S(1)} %fusion.82, f32[256,256]{1,0:T(8,128)S(1)} %fusion.83), kind=kOutput, calls=%fused_computation.2.clone.1 | convolution fusion | flops 1611661312 | bytes 6553600 | tf_op jit(solution)/shard_map/while/body/eval_jaxpr/pij,pjk->pik/dot_general | solution.py:11
  225.8 4.9 %fusion.84 = f32[8,256,256]{1,2,0:T(8,128)} fusion(f32[8,256,256]{1,2,0:T(8,128)S(1)} %copy.88, f32[8,256,256]{2,1,0:T(8,128)S(1)} %fusion.82, f32[256,256]{1,0:T(8,128)S(1)} %fusion.83), kind=kOutput, calls=%fused_computation.4.clone.1 | convolution fusion | flops 1611661312 | bytes 6553600 | tf_op jit(solution)/shard_map/while/body/eval_jaxpr/pij,pjk->pik/dot_general | solution.py:11
  233.2 2.2 fusion.82
  235.4 3.6 %fusion.85 = f32[8,256,256]{2,1,0:T(8,128)} fusion(f32[8,256,256]{2,1,0:T(8,128)S(1)} %copy.89, f32[8,256,256]{2,1,0:T(8,128)S(1)} %fusion.82, f32[256,256]{1,0:T(8,128)S(1)} %fusion.83), kind=kOutput, calls=%fused_computation.2.clone.1 | convolution fusion | flops 1611661312 | bytes 6553600 | tf_op jit(solution)/shard_map/while/body/eval_jaxpr/pij,pjk->pik/dot_general | solution.py:11
  238.9 4.9 %fusion.84 = f32[8,256,256]{1,2,0:T(8,128)} fusion(f32[8,256,256]{1,2,0:T(8,128)S(1)} %copy.88, f32[8,256,256]{2,1,0:T(8,128)S(1)} %fusion.82, f32[256,256]{1,0:T(8,128)S(1)} %fusion.83), kind=kOutput, calls=%fused_computation.4.clone.1 | convolution fusion | flops 1611661312 | bytes 6553600 | tf_op jit(solution)/shard_map/while/body/eval_jaxpr/pij,pjk->pik/dot_general | solution.py:11
  246.3 2.2 fusion.82
  248.5 3.6 %fusion.85 = f32[8,256,256]{2,1,0:T(8,128)} fusion(f32[8,256,256]{2,1,0:T(8,128)S(1)} %copy.89, f32[8,256,256]{2,1,0:T(8,128)S(1)} %fusion.82, f32[256,256]{1,0:T(8,128)S(1)} %fusion.83), kind=kOutput, calls=%fused_computation.2.clone.1 | convolution fusion | flops 1611661312 | bytes 6553600 | tf_op jit(solution)/shard_map/while/body/eval_jaxpr/pij,pjk->pik/dot_general | solution.py:11
  252.0 4.9 %fusion.84 = f32[8,256,256]{1,2,0:T(8,128)} fusion(f32[8,256,256]{1,2,0:T(8,128)S(1)} %copy.88, f32[8,256,256]{2,1,0:T(8,128)S(1)} %fusion.82, f32[256,256]{1,0:T(8,128)S(1)} %fusion.83), kind=kOutput, calls=%fused_computation.4.clone.1 | convolution fusion | flops 1611661312 | bytes 6553600 | tf_op jit(solution)/shard_map/while/body/eval_jaxpr/pij,pjk->pik/dot_general | solution.py:11
  256.9 3.7 %fusion.58 = f32[8,1,256]{2,1,0:T(1,128)S(1)} fusion(f32[8,256,1]{1,0,2:T(8,128)S(1)} %bitcast.115, f32[8,256,256]{2,1,0:T(8,128)} %get-tuple-element.24, f32[8]{0:T(128)S(1)} %sqrt.7), kind=kOutput, calls=%fused_computation.78 | convolution fusion | flops 6815744 | bytes 2113568 | tf_op jit(solution)/shard_map/pij,pj->pi/dot_general | solution.py:70
  260.7 2.0 fusion.56
  262.7 4.0 %add_bitcast_fusion = f32[256,8,256]{0,2,1:T(8,128)} fusion(f32[256,8,256]{0,2,1:T(8,128)S(1)} %copy-done.3, f32[8,256]{1,0:T(8,128)S(1)} %bitcast.116, f32[8,256]{1,0:T(8,128)S(1)} %broadcast_multiply_fusion.1, f32[8,256,256]{2,1,0:T(8,128)S(1)} %copy-done.2, f32[8]{0:T(128)S(1)} %sqrt.7), kind=kOutput, calls=%fused_computation.24 | convolution fusion | flops 1613234176 | bytes 6307872 | tf_op jit(solution)/shard_map/pjk,jpc->kpc/dot_general | solution.py:75
  266.7 3.0 copy.33
  269.7 4.3 %all-to-all-start.1 = ((f32[256,8,256]{2,1,0:T(8,128)}), f32[256,8,256]{2,1,0:T(8,128)}, u32[]{:S(2)}, u32[]{:S(2)}) async-start(f32[256,8,256]{2,1,0:T(8,128)} %copy.33), calls=%async_computation.1 | async-start | bytes 4194304 | tf_op jit(solution)/shard_map/all_to_all | solution.py:76
  274.1 3.2 multiply_bitcast_fusion
  277.3 44.6 %all-to-all-done.1 = f32[256,8,256]{2,1,0:T(8,128)} async-done(((f32[256,8,256]{2,1,0:T(8,128)}), f32[256,8,256]{2,1,0:T(8,128)}, u32[]{:S(2)}, u32[]{:S(2)}) %all-to-all-start.1) | async-done | bytes 2097184 | tf_op jit(solution)/shard_map/all_to_all | solution.py:76
  321.9 4.1 %fusion.32 = f32[32,64,256]{2,1,0:T(8,128)} fusion(f32[32,8,8,256]{3,2,0,1:T(8,128)} %bitcast.27, s32[64]{0:T(128)S(1)} %bitcast.121), kind=kOutput, calls=%fused_computation.36 | convolution fusion | flops 402657280 | bytes 4194560 | tf_op jit(solution)/shard_map/kjc,qj->kqc/dot_general | solution.py:77
  (90 shorter events, 28.8 us)
Async XLA Ops:
  0.6 1.6 copy-start
  9.9 8.2 %copy-start.5 = (f32[1,8,512]{2,1,0:T(8,128)S(1)}, f32[1,8,512]{2,1,0:T(8,128)}, u32[]{:S(2)}) copy-start(f32[1,8,512]{2,1,0:T(8,128)} %param.15) | copy-start | bytes 49156
  9.9 8.3 %copy-start.7 = (s32[1,8]{1,0:T(1,128)S(1)}, s32[1,8]{1,0:T(1,128)}, u32[]{:S(2)}) copy-start(s32[1,8]{1,0:T(1,128)} %param.13) | copy-start | bytes 100
  9.9 55.8 %all-to-all-start = ((f32[8,32,8,256]{3,2,1,0:T(8,128)}), f32[8,32,8,256]{3,2,1,0:T(8,128)}, u32[]{:S(2)}, u32[]{:S(2)}) async-start(f32[8,32,8,256]{3,2,1,0:T(8,128)} %fusion.38), calls=%async_computation | async-start | bytes 4194304 | tf_op jit(solution)/shard_map/all_to_all | solution.py:42
  70.4 2.6 copy-start.4
  80.7 4.3 %copy-start.6 = (f32[1,8,512]{2,1,0:T(8,128)S(1)}, f32[1,8,512]{2,1,0:T(8,128)}, u32[]{:S(2)}) copy-start(f32[1,8,512]{2,1,0:T(8,128)} %param.14) | copy-start | bytes 49156
  99.6 2.2 copy-start.1
  112.7 2.2 copy-start.1
  125.8 2.2 copy-start.1
  138.9 2.2 copy-start.1
  152.0 2.2 copy-start.1
  165.2 2.2 copy-start.1
  178.3 2.2 copy-start.1
  191.4 2.2 copy-start.1
  204.5 2.2 copy-start.1
  217.6 2.2 copy-start.1
  230.7 2.2 copy-start.1
  243.8 2.2 copy-start.1
  256.9 3.7 %copy-start.2 = (f32[8,256,256]{2,1,0:T(8,128)S(1)}, f32[8,256,256]{2,1,0:T(8,128)}, u32[]{:S(2)}) copy-start(f32[8,256,256]{2,1,0:T(8,128)} %get-tuple-element.24) | copy-start | bytes 6291460
  260.7 2.0 copy-start.3
  269.7 52.2 %all-to-all-start.1 = ((f32[256,8,256]{2,1,0:T(8,128)}), f32[256,8,256]{2,1,0:T(8,128)}, u32[]{:S(2)}, u32[]{:S(2)}) async-start(f32[256,8,256]{2,1,0:T(8,128)} %copy.33), calls=%async_computation.1 | async-start | bytes 4194304 | tf_op jit(solution)/shard_map/all_to_all | solution.py:76
  274.1 47.8 %copy-start.8 = (s32[1,64]{1,0:T(1,128)S(1)}, s32[1,64]{1,0:T(1,128)}, u32[]{:S(2)}) copy-start(s32[1,64]{1,0:T(1,128)} %param.11) | copy-start | bytes 772
